TPU v7x, 32 devices: a whole 2x2x4 slice. The times are simulated.
32 devices in a mesh: parts: 2 (over y), seq: 4 (over z), head: 4 (over x, core).
Axes of the slice: x: 2, y: 2, z: 4, core: 2. Of those that a mesh axis runs over, the one named last changes fastest.
Arguments:
- hidden: bfloat16 [48, 12288], P(('parts', 'head'), 'seq'), parts along dimension 0, may hold values from -600 to 600
- norm_gain: float32 [12288], P('seq'), may hold values from 0.1 to 1.9
- w_query: bfloat16 [12288, 12288], P('seq', 'head'), may hold values from -0.0546875 to 0.0546875
- w_key: bfloat16 [12288, 1024], P('seq', 'head'), may hold values from -0.0546875 to 0.0546875
- w_value: bfloat16 [12288, 1024], P('seq', 'head'), may hold values from -0.0546875 to 0.0546875
- w_out: bfloat16 [12288, 12288], P('head', 'seq'), may hold values from -0.0546875 to 0.0546875
- lengths: int32 [48], P('parts'), parts along dimension 0, may hold values from 1 to 512, as said below
- key_cache: bfloat16 [48, 8, 512, 128], P('parts', 'head', 'seq'), parts along dimension 0, may hold values from -600 to 600, as said below
- value_cache: bfloat16 [48, 8, 512, 128], P('parts', 'head', 'seq'), parts along dimension 0, may hold values from -6 to 6
Outputs:
- attn_out: bfloat16 [48, 12288], P(('parts', 'head'), 'seq'), parts along dimension 0
There are 2 independent parts, one for each index of `parts`. A program takes and returns all parts, laid end to end along the dimension named above; an argument that names none is the same for every part. Nothing has to cross between parts.
Inputs may be any that keep to these rules, and one draw needn't show every extreme that they name: Sequence b holds lengths[b] cached tokens at positions 0 to lengths[b] - 1; its new token takes position lengths[b]. `key_cache`: positions at or past a sequence's length hold no data.
All inputs are finite; a program needn't handle non-finite values.
Results may differ from a plain program's by a relative error of at most 0.0075.
The roundings to bfloat16 on the way count: a program that leaves them out, or rounds other values in their place, can miss the bound.
Values may be sent and summed in bfloat16 or wider, within the bound.
A program may use at most 128 MiB of HBM per device.

v0:
```python
import jax
import jax.numpy as jnp
from jax import lax
from jax.sharding import PartitionSpec as P

D = 12288
EPSILON = 1e-05


def joined(value, axis, join):
    pieces = jax.tree.map(lambda part: lax.all_gather(part, axis), value)
    head = jax.tree.map(lambda part: part[0], pieces)
    tail = jax.tree.map(lambda part: part[1:], pieces)
    subtotal, _ = lax.scan(lambda subtotal, slab: (join(subtotal, slab), None), head, tail)
    return subtotal


def join_parts(earlier, later):
    new_max = jnp.maximum(earlier[0], later[0])
    left_factor = jnp.exp(earlier[0] - new_max)
    right_factor = jnp.exp(later[0] - new_max)
    den_total = earlier[1] * left_factor + later[1] * right_factor
    acc_total = earlier[2] * left_factor[..., None] + later[2] * right_factor[..., None]
    return (new_max, den_total, acc_total)


def local(hidden, norm_gain, w_query, w_key, w_value, w_out, lengths, key_cache, value_cache):
    batch_size, kv_local, block_len, head_size = key_cache.shape
    group_size = w_query.shape[1] // (kv_local * head_size)
    token_rows = lax.all_gather(hidden, "head", axis=0, tiled=True)
    widened = token_rows.astype(jnp.float32)
    square_local = jnp.sum(widened * widened, axis=1)
    scaled = (widened * norm_gain).astype(jnp.bfloat16)
    query_part = jnp.dot(scaled, w_query, preferred_element_type=jnp.float32)
    key_part = jnp.dot(scaled, w_key, preferred_element_type=jnp.float32)
    value_part = jnp.dot(scaled, w_value, preferred_element_type=jnp.float32)
    query_factor = float(head_size) ** (-0.5)
    norm_total = lax.psum(square_local, "seq")
    query_sum, key_sum, value_sum = lax.psum((query_part, key_part, value_part), "seq")
    inverse_rms = lax.rsqrt(norm_total / D + EPSILON)[:, None]
    queries = (query_sum * inverse_rms * query_factor).astype(jnp.bfloat16)
    new_keys = (key_sum * inverse_rms).astype(jnp.bfloat16)
    new_values = (value_sum * inverse_rms).astype(jnp.bfloat16)
    grouped = queries.reshape(batch_size, kv_local, group_size, head_size)
    scores = jnp.einsum("bkgd,bkpd->bkgp", grouped, key_cache, preferred_element_type=jnp.float32)
    offset = lax.axis_index("seq") * block_len
    positions = offset + jnp.arange(block_len, dtype=jnp.int32)
    live_mask = (positions[None, :] < lengths[:, None])[:, None, None, :]
    block_max = jnp.max(jnp.where(live_mask, scores, -1e30), axis=-1)
    shifted = jnp.where(live_mask, scores - block_max[..., None], 0.0)
    weights = jnp.where(live_mask, jnp.exp(shifted), 0.0).astype(jnp.bfloat16)
    block_den = jnp.sum(weights.astype(jnp.float32), axis=-1)
    block_acc = jnp.einsum(
        "bkgp,bkpd->bkgd", weights, value_cache, preferred_element_type=jnp.float32
    )
    self_score = jnp.einsum(
        "oips,ois->oip",
        grouped,
        new_keys.reshape(batch_size, kv_local, head_size),
        preferred_element_type=jnp.float32,
    )
    global_max, den_merged, acc_merged = joined(
        (block_max, block_den, block_acc), "seq", join_parts
    )
    top_score = jnp.maximum(global_max, self_score)
    factors = jnp.exp(global_max - top_score)
    den_sum = den_merged * factors
    acc_sum = acc_merged * factors[..., None]
    own_weight = jnp.exp(self_score - top_score)
    denominator = den_sum + own_weight
    numerator = acc_sum + own_weight[..., None] * new_values.reshape(
        batch_size, kv_local, 1, head_size
    ).astype(jnp.float32)
    mixed = (
        (numerator / denominator[..., None])
        .astype(jnp.bfloat16)
        .reshape(batch_size, kv_local * group_size * head_size)
    )
    output = lax.psum_scatter(
        jnp.dot(mixed, w_out, preferred_element_type=jnp.float32),
        "head",
        scatter_dimension=0,
        tiled=True,
    )
    return output.astype(jnp.bfloat16)


def solution(mesh):
    return jax.shard_map(
        local,
        mesh=mesh,
        in_specs=(
            P(("parts", "head"), "seq"),
            P("seq"),
            P("seq", "head"),
            P("seq", "head"),
            P("seq", "head"),
            P("head", "seq"),
            P("parts"),
            P("parts", "head", "seq", None),
            P("parts", "head", "seq", None),
        ),
        out_specs=P(("parts", "head"), "seq"),
        check_vma=False,
    )
```

profile of v0, /device:TPU:1, one launch (start us, length us, event | category | flops | bytes accessed | tf_op | source)
XLA Modules:
  0.0 132.5 jit_solution(6576906076258920298)
XLA Ops:
  6.5 7.0 %all-gather.3 = bf16[4,6,3072]{2,1,0:T(8,128)(2,1)S(1)} all-gather(bf16[1,6,3072]{2,1,0:T(8,128)(2,1)} %bitcast.49), channel_id=1, replica_groups=mesh['parts'=2,'seq'=4,'head'=4] {'head'}, dimensions={0}, use_global_device_ids=true | all-gather | bytes 184320 | tf_op jit(solution)/shard_map/all_gather | solution.py:30
  13.6 0.9 multiply_reduce_fusion
  14.5 9.8 %fusion.12 = f32[24,3072]{1,0:T(8,128)} fusion(bf16[24,3072]{1,0:T(8,128)(2,1)S(1)} %get-tuple-element.86, bf16[3072,3072]{1,0:T(8,128)(2,1)} %param.13), kind=kOutput, calls=%fused_computation.30 | convolution fusion | flops 452984832 | bytes 19316736 | tf_op jit(solution)/shard_map/dot_general | solution.py:34
  24.7 1.1 copy-done.2
  26.1 17.1 %all-reduce.2 = (f32[24]{0:T(128)S(1)}, f32[24,256]{1,0:T(8,128)S(1)}, f32[24,256]{1,0:T(8,128)S(1)}) all-reduce(f32[24]{0:T(128)S(1)} %get-tuple-element.85, f32[24,256]{1,0:T(8,128)S(1)} %fusion.13, f32[24,256]{1,0:T(8,128)S(1)} %fusion.15), channel_id=1, replica_groups=mesh['parts'=2,'seq'=4,'head'=4] {'seq'}, use_global_device_ids=true, to_apply=%region_2.0 | all-reduce | flops 12312 | bytes 98496 | tf_op jit(solution)/shard_map/psum | solution.py:38
  43.3 16.5 %all-reduce.5.cloned.1.call-done = f32[24,3072]{1,0:T(8,128)} async-done(((f32[24,3072]{1,0:T(8,128)}), f32[24,3072]{1,0:T(8,128)}) %all-reduce.5.cloned.1.call-update) | async-done | bytes 294928 | tf_op jit(solution)/shard_map/psum | solution.py:39
  59.8 1.1 multiply_convert_fusion
  61.0 1.0 select_reduce_fusion
  62.0 2.0 %fusion.8 = f32[24,2,12,128]{3,2,1,0:T(8,128)S(1)} fusion(bf16[24,2,128,128]{3,2,1,0:T(8,128)(2,1)} %param.19, f32[24,2,12,128]{3,2,1,0:T(8,128)S(1)} %get-tuple-element.90, f32[24,2,12]{2,1,0:T(2,128)S(1)} %get-tuple-element.89, pred[24,128]{1,0:T(8,128)(4,1)S(1)} %broadcast_compare_fusion), kind=kOutput, calls=%fused_computation.29 | convolution fusion | flops 19169280 | bytes 2168064 | tf_op jit(solution)/shard_map/bkgp,bkpd->bkgd/dot_general | solution.py:53
  64.0 0.9 copy.26
  65.0 10.4 %all-gather = f32[96,2,12]{2,1,0:T(2,128)S(1)} all-gather(f32[24,2,12]{2,1,0:T(2,128)S(1)} %get-tuple-element.89), channel_id=2, replica_groups=mesh['parts'=2,'seq'=4,'head'=4] {'seq'}, dimensions={0}, use_global_device_ids=true | all-gather | bytes 11520 | tf_op jit(solution)/shard_map/all_gather | solution.py:11
  75.8 11.5 %all-gather.1 = f32[96,2,12]{2,1,0:T(2,128)S(1)} all-gather(f32[24,2,12]{2,1,0:T(2,128)S(1)} %convert_reduce_fusion), channel_id=3, replica_groups=mesh['parts'=2,'seq'=4,'head'=4] {'seq'}, dimensions={0}, use_global_device_ids=true | all-gather | bytes 11520 | tf_op jit(solution)/shard_map/all_gather | solution.py:11
  88.0 10.4 %all-gather.6.cloned.1.call-done = f32[96,2,12,128]{3,1,2,0:T(2,128)} async-done(((f32[24,2,12,128]{3,1,2,0:T(2,128)}), f32[96,2,12,128]{3,1,2,0:T(2,128)}) %all-gather.6.cloned.1.call-update) | async-done | bytes 1179664 | tf_op jit(solution)/shard_map/all_gather | solution.py:11
  98.5 1.1 slice.32
  99.7 2.0 %while.14 = (s32[]{:T(128)}, f32[24,2,12]{0,1,2:T(2,128)S(1)}, f32[24,2,12]{0,1,2:T(2,128)S(1)}, f32[24,2,12,128]{3,2,1,0:T(8,128)S(1)}, f32[3,24,2,12]{1,2,3,0:...) while((s32[]{:T(128)}, f32[24,2,12]{0,1,2:T(2,128)S(1)}, ...), condition=%wide.region_6.7_spmd, body=%wide.region_5.6_spmd.sunk | while | flops 224642 | bytes 1506917 | solution.py:14
  100.0 0.4 fusion.33
  100.7 0.4 fusion.33
  101.3 0.4 fusion.33
  102.0 0.4 divide_convert_fusion
  102.5 7.7 %fusion.16 = f32[24,3072]{1,0:T(8,128)S(1)} fusion(bf16[24,3072]{1,0:T(8,128)(2,1)S(1)} %reshape.56, bf16[3072,3072]{1,0:T(8,128)(2,1)} %param.16), kind=kOutput, calls=%fused_computation.34 | convolution fusion | flops 452984832 | bytes 19316736 | tf_op jit(solution)/shard_map/dot_general | solution.py:80
  110.2 9.0 %fusion = f32[8,3072]{1,0:T(8,128)S(1)} fusion(f32[24,3072]{1,0:T(8,128)S(1)} %fusion.16), kind=kCustom, calls=%all-reduce-scatter | all-reduce-scatter fusion | flops 98305 | bytes 393728
  119.2 4.3 %collective-permute-start = (bf16[6,3072]{1,0:T(8,128)(2,1)S(1)}, bf16[6,3072]{1,0:T(8,128)(2,1)S(1)}, u32[]{:S(2)}, u32[]{:S(2)}) collective-permute-start(bf16[6,3072]{1,0:T(8,128)(2,1)S(1)} %slice.36), channel_id=1, source_target_pairs={{0,1},{1,2},{2,3},{4,5},{5,6},{6,7},{8,9},{9,10},{10,11},{12,13},{... | collective-permute-start | bytes 110600
  123.6 0.6 dynamic-slice.4
  125.0 0.6 dynamic-slice_convert_fusion
  (57 shorter events, 3.8 us)
Async XLA Ops:
  6.5 54.4 %copy-start = (bf16[24,2,128,128]{3,2,1,0:T(8,128)(2,1)S(1)}, bf16[24,2,128,128]{3,2,1,0:T(8,128)(2,1)}, u32[]{:S(2)}) copy-start(bf16[24,2,128,128]{3,2,1,0:T(8,128)(2,1)} %param.18) | copy-start | bytes 4718596
  6.5 53.2 %all-reduce.5.cloned.1.call-start = ((), (), s32[]{:S(2)}) async-start(), calls=%async_computation | async-start | bytes 589824 | tf_op jit(solution)/shard_map/psum | solution.py:39
  14.5 9.8 %copy-start.1 = (bf16[3072,256]{1,0:T(8,128)(2,1)S(1)}, bf16[3072,256]{1,0:T(8,128)(2,1)}, u32[]{:S(2)}) copy-start(bf16[3072,256]{1,0:T(8,128)(2,1)} %param.15) | copy-start | bytes 4718596
  24.3 74.2 %all-gather.6.cloned.1.call-start = ((), (), s32[]{:S(2)}) async-start(), calls=%async_computation.1 | async-start | bytes 1474560 | tf_op jit(solution)/shard_map/all_gather | solution.py:11
  24.3 1.4 %copy-start.2 = (bf16[3072,256]{1,0:T(8,128)(2,1)S(1)}, bf16[3072,256]{1,0:T(8,128)(2,1)}, u32[]{:S(2)}) copy-start(bf16[3072,256]{1,0:T(8,128)(2,1)} %param.14) | copy-start | bytes 4718596
  24.4 18.9 %copy-start.4 = (s32[24]{0:T(128)S(1)}, s32[24]{0:T(128)}, u32[]{:S(2)}) copy-start(s32[24]{0:T(128)} %param.17) | copy-start | bytes 292
  98.5 1.3 slice-start
  102.5 21.0 %copy-start.3 = (u32[32]{0:T(128)S(1)}, u32[32]{0:T(128)}, u32[]{:S(2)}) copy-start(u32[32]{0:T(128)} %constant.37) | copy-start | bytes 388
  119.2 5.6 %collective-permute-start = (bf16[6,3072]{1,0:T(8,128)(2,1)S(1)}, bf16[6,3072]{1,0:T(8,128)(2,1)S(1)}, u32[]{:S(2)}, u32[]{:S(2)}) collective-permute-start(bf16[6,3072]{1,0:T(8,128)(2,1)S(1)} %slice.36), channel_id=1, source_target_pairs={{0,1},{1,2},{2,3},{4,5},{5,6},{6,7},{8,9},{9,10},{10,11},{12,13},{... | collective-permute-start | bytes 110600
Sparse Core Ops, SparseCore 0:
  24.4 35.3 all-reduce.4
  65.0 33.4 all-gather.5
where the time goes:
time: 133 us; the launch traced here: 132 us
  blocking collectives  55.1 us (41%)
  waiting for transfers between devices  26.9 us (20%)
  matrix products  21.3 us (16%)
  between operations  14.3 us (11%)
  local copies, waits for them, and re-layouts  6.41 us (5%)
  starting transfers between devices  4.35 us (3%)
  other arithmetic  4.09 us (3%)
    all_gather x2, blocking collectives, joined(): pieces = jax.tree.map(lambda part: lax.all_gather(part, axis), value)  21.9 us
    psum x1, blocking collectives, local(): norm_total = lax.psum(square_local, 'seq')  17.1 us
    psum x1, waiting for transfers between devices, local(): lax.psum((query_part, key_part, value_part), 'seq')  16.5 us
    all_gather x1, waiting for transfers between devices, joined(): pieces = jax.tree.map(lambda part: lax.all_gather(part, axis), value)  10.4 us
    dot_general x1, matrix products, local(): query_part = jnp.dot(scaled, w_query, preferred_element_type=jnp.float32)  9.76 us
    unnamed x1, blocking collectives  8.98 us
    dot_general x1, matrix products, local(): jnp.dot(mixed, w_out, preferred_element_type=jnp.float32)  7.7 us
    all_gather x1, blocking collectives, local(): token_rows = lax.all_gather(hidden, 'head', axis=0, tiled=True)  7.05 us
  transfers between devices with their start and end apart: 3, of which 2 were waited for; matrix products, arithmetic and copies ran while one was open for 2% of the time, Pallas kernels for 0%

commit v1 on v0

--- a/solution.py
+++ b/solution.py
@@ -35,7 +35,11 @@
     key_part = jnp.dot(scaled, w_key, preferred_element_type=jnp.float32)
     value_part = jnp.dot(scaled, w_value, preferred_element_type=jnp.float32)
     query_factor = float(head_size) ** (-0.5)
-    norm_total = lax.psum(square_local, "seq")
+    norm_total = square_local
+    for hop in (1, 2):
+        norm_total = norm_total + lax.ppermute(
+            norm_total, "seq", [(dev, dev ^ hop) for dev in range(4)]
+        )
     query_sum, key_sum, value_sum = lax.psum((query_part, key_part, value_part), "seq")
     inverse_rms = lax.rsqrt(norm_total / D + EPSILON)[:, None]
     queries = (query_sum * inverse_rms * query_factor).astype(jnp.bfloat16)

time: 133 us -> 149 us (1.12)
  blocking collectives: 55.1 us -> 63.8 us
  waiting for transfers between devices: 26.9 us -> 31.4 us
  starting transfers between devices: 4.35 us -> 8.29 us
    psum x1, waiting for transfers between devices: 16.5 us -> 30.4 us  [local(): lax.psum((query_part, key_part, value_part), 'seq')]
    all_gather x1, waiting for transfers between devices: 10.4 us -> 0.02 us  [joined(): pieces = jax.tree.map(lambda part: lax.all_gather(part, axis), value)]
    unnamed x1, blocking collectives: 8.98 us -> 18.1 us
    ppermute x0 -> x2, starting transfers between devices: none -> 3.94 us  [local(): lax.ppermute(norm_total, 'seq', [(dev, dev ^ hop) for dev in range(4)])]
    dot_general x1, matrix products: 0.32 us -> 1.84 us  [local(): value_part = jnp.dot(scaled, w_value, preferred_element_type=jnp.float32)]
  transfers between devices with their start and end apart: 3 -> 5, of which waited for: 2 -> 2; matrix products, arithmetic and copies ran while one was open for 2% -> 9% of each run, Pallas kernels for 0% -> 0%
where the time goes in v1:
time: 149 us
  blocking collectives  63.8 us (43%)
  waiting for transfers between devices  31.4 us (21%)
  matrix products  21.3 us (14%)
  between operations  14.3 us (10%)
  starting transfers between devices  8.29 us (6%)
  local copies, waits for them, and re-layouts  5.77 us (4%)
  other arithmetic  4.09 us (3%)
    psum x1, waiting for transfers between devices, local(): lax.psum((query_part, key_part, value_part), 'seq')  30.4 us
    all_gather x2, blocking collectives, joined(): pieces = jax.tree.map(lambda part: lax.all_gather(part, axis), value)  22.4 us
    unnamed x1, blocking collectives  18.1 us
    psum x1, blocking collectives, local(): lax.psum((query_part, key_part, value_part), 'seq')  16.3 us
    dot_general x1, matrix products, local(): query_part = jnp.dot(scaled, w_query, preferred_element_type=jnp.float32)  9.65 us
    dot_general x1, matrix products, local(): jnp.dot(mixed, w_out, preferred_element_type=jnp.float32)  7.7 us
    all_gather x1, blocking collectives, local(): token_rows = lax.all_gather(hidden, 'head', axis=0, tiled=True)  7.05 us
    unnamed x1, starting transfers between devices  4.3 us
  transfers between devices with their start and end apart: 5, of which 2 were waited for; matrix products, arithmetic and copies ran while one was open for 9% of the time, Pallas kernels for 0%

profile of v1, /device:TPU:1, one launch (start us, length us, event | category | flops | bytes accessed | tf_op | source)
XLA Modules:
  0.0 149.0 jit_solution(6374439148872609451)
XLA Ops:
  6.5 7.0 %all-gather.3 = bf16[4,6,3072]{2,1,0:T(8,128)(2,1)S(1)} all-gather(bf16[1,6,3072]{2,1,0:T(8,128)(2,1)} %bitcast.49), channel_id=1, replica_groups=mesh['parts'=2,'seq'=4,'head'=4] {'head'}, dimensions={0}, use_global_device_ids=true | all-gather | bytes 184320 | tf_op jit(solution)/shard_map/all_gather | solution.py:30
  13.6 0.9 multiply_reduce_fusion
  14.5 1.6 %collective-permute-start = (f32[24]{0:T(128)S(1)}, f32[24]{0:T(128)S(1)}, u32[]{:S(2)}, u32[]{:S(2)}) collective-permute-start(f32[24]{0:T(128)S(1)} %get-tuple-element.84), channel_id=1, source_target_pairs={{0,4},{4,0},{8,12},{12,8},{1,5},{5,1},{9,13},{13,9},{2,6},{6,2},{1... | collective-permute-start | bytes 296 | tf_op jit(solution)/shard_map/ppermute | solution.py:40
  16.1 9.7 %fusion.12 = f32[24,3072]{1,0:T(8,128)} fusion(bf16[24,3072]{1,0:T(8,128)(2,1)S(1)} %get-tuple-element.85, bf16[3072,3072]{1,0:T(8,128)(2,1)} %param.13), kind=kOutput, calls=%fused_computation.30 | convolution fusion | flops 452984832 | bytes 19316736 | tf_op jit(solution)/shard_map/dot_general | solution.py:34
  25.8 2.4 %collective-permute-start.1 = (f32[24]{0:T(128)S(1)}, f32[24]{0:T(128)S(1)}, u32[]{:S(2)}, u32[]{:S(2)}) collective-permute-start(f32[24]{0:T(128)S(1)} %add.44), channel_id=1, source_target_pairs={{0,8},{4,12},{8,0},{12,4},{1,9},{5,13},{9,1},{13,5},{2,10},{6,14},... | collective-permute-start | bytes 296 | tf_op jit(solution)/shard_map/ppermute | solution.py:40
  28.3 0.9 collective-permute-done.1
  29.2 30.4 %all-reduce.5.cloned.1.call-done = f32[24,3072]{1,0:T(8,128)} async-done(((f32[24,3072]{1,0:T(8,128)}), f32[24,3072]{1,0:T(8,128)}) %all-reduce.5.cloned.1.call-update) | async-done | bytes 294928 | tf_op jit(solution)/shard_map/psum | solution.py:43
  59.6 1.1 multiply_convert_fusion
  60.8 1.0 select_reduce_fusion
  61.8 0.4 copy-done.4
  62.2 0.6 fusion.8
  62.8 0.9 copy.26
  63.8 1.8 %fusion.15 = f32[24,256]{1,0:T(8,128)S(1)} fusion(bf16[24,3072]{1,0:T(8,128)(2,1)S(1)} %get-tuple-element.85, bf16[3072,256]{1,0:T(8,128)(2,1)} %param.15), kind=kOutput, calls=%fused_computation.33 | convolution fusion | flops 37748736 | bytes 1744896 | tf_op jit(solution)/shard_map/dot_general | solution.py:36
  66.0 16.3 %all-reduce.2 = (f32[24,256]{1,0:T(8,128)S(1)}, f32[24,256]{1,0:T(8,128)S(1)}) all-reduce(f32[24,256]{1,0:T(8,128)S(1)} %fusion.13, f32[24,256]{1,0:T(8,128)S(1)} %fusion.15), channel_id=1, replica_groups=mesh['parts'=2,'seq'=4,'head'=4] {'seq'}, use_global_device_ids=true, to_apply=%region_6.7 | all-reduce | flops 12288 | bytes 98304 | tf_op jit(solution)/shard_map/psum | solution.py:43
  82.3 12.0 %all-gather = f32[96,2,12]{2,1,0:T(2,128)S(1)} all-gather(f32[24,2,12]{2,1,0:T(2,128)S(1)} %get-tuple-element.88), channel_id=2, replica_groups=mesh['parts'=2,'seq'=4,'head'=4] {'seq'}, dimensions={0}, use_global_device_ids=true | all-gather | bytes 11520 | tf_op jit(solution)/shard_map/all_gather | solution.py:11
  94.7 10.4 %all-gather.1 = f32[96,2,12]{2,1,0:T(2,128)S(1)} all-gather(f32[24,2,12]{2,1,0:T(2,128)S(1)} %convert_reduce_fusion), channel_id=3, replica_groups=mesh['parts'=2,'seq'=4,'head'=4] {'seq'}, dimensions={0}, use_global_device_ids=true | all-gather | bytes 11520 | tf_op jit(solution)/shard_map/all_gather | solution.py:11
  105.9 1.1 slice.32
  107.1 2.0 %while.14 = (s32[]{:T(128)}, f32[24,2,12]{0,1,2:T(2,128)S(1)}, f32[24,2,12]{0,1,2:T(2,128)S(1)}, f32[24,2,12,128]{3,2,1,0:T(8,128)S(1)}, f32[3,24,2,12]{1,2,3,0:...) while((s32[]{:T(128)}, f32[24,2,12]{0,1,2:T(2,128)S(1)}, ...), condition=%wide.region_5.6_spmd, body=%wide.region_4.5_spmd.sunk | while | flops 224642 | bytes 1506917 | solution.py:14
  107.4 0.4 fusion.33
  109.9 7.7 %fusion.16 = f32[24,3072]{1,0:T(8,128)S(1)} fusion(bf16[24,3072]{1,0:T(8,128)(2,1)S(1)} %reshape.56, bf16[3072,3072]{1,0:T(8,128)(2,1)} %param.16), kind=kOutput, calls=%fused_computation.34 | convolution fusion | flops 452984832 | bytes 19316736 | tf_op jit(solution)/shard_map/dot_general | solution.py:84
  117.6 18.1 %fusion = f32[8,3072]{1,0:T(8,128)S(1)} fusion(f32[24,3072]{1,0:T(8,128)S(1)} %fusion.16), kind=kCustom, calls=%all-reduce-scatter | all-reduce-scatter fusion | flops 98305 | bytes 393728
  135.8 4.3 %collective-permute-start.2 = (bf16[6,3072]{1,0:T(8,128)(2,1)S(1)}, bf16[6,3072]{1,0:T(8,128)(2,1)S(1)}, u32[]{:S(2)}, u32[]{:S(2)}) collective-permute-start(bf16[6,3072]{1,0:T(8,128)(2,1)S(1)} %slice.36), channel_id=1, source_target_pairs={{0,1},{1,2},{2,3},{4,5},{5,6},{6,7},{8,9},{9,10},{10,11},{12,13},{... | collective-permute-start | bytes 110600
  140.1 0.6 dynamic-slice.4
  141.6 0.6 dynamic-slice_convert_fusion
  (62 shorter events, 4.6 us)
Async XLA Ops:
  6.5 54.3 %copy-start = (bf16[24,2,128,128]{3,2,1,0:T(8,128)(2,1)S(1)}, bf16[24,2,128,128]{3,2,1,0:T(8,128)(2,1)}, u32[]{:S(2)}) copy-start(bf16[24,2,128,128]{3,2,1,0:T(8,128)(2,1)} %param.18) | copy-start | bytes 4718596
  6.5 53.1 %all-reduce.5.cloned.1.call-start = ((), (), s32[]{:S(2)}) async-start(), calls=%async_computation | async-start | bytes 589824 | tf_op jit(solution)/shard_map/psum | solution.py:43
  14.5 11.3 %collective-permute-start = (f32[24]{0:T(128)S(1)}, f32[24]{0:T(128)S(1)}, u32[]{:S(2)}, u32[]{:S(2)}) collective-permute-start(f32[24]{0:T(128)S(1)} %get-tuple-element.84), channel_id=1, source_target_pairs={{0,4},{4,0},{8,12},{12,8},{1,5},{5,1},{9,13},{13,9},{2,6},{6,2},{1... | collective-permute-start | bytes 296 | tf_op jit(solution)/shard_map/ppermute | solution.py:40
  16.1 12.1 %copy-start.3 = (s32[24]{0:T(128)S(1)}, s32[24]{0:T(128)}, u32[]{:S(2)}) copy-start(s32[24]{0:T(128)} %param.17) | copy-start | bytes 292
  25.7 80.1 %all-gather.6.cloned.1.call-start = ((), (), s32[]{:S(2)}) async-start(), calls=%async_computation.1 | async-start | bytes 1474560 | tf_op jit(solution)/shard_map/all_gather | solution.py:11
  25.8 3.4 %collective-permute-start.1 = (f32[24]{0:T(128)S(1)}, f32[24]{0:T(128)S(1)}, u32[]{:S(2)}, u32[]{:S(2)}) collective-permute-start(f32[24]{0:T(128)S(1)} %add.44), channel_id=1, source_target_pairs={{0,8},{4,12},{8,0},{12,4},{1,9},{5,13},{9,1},{13,5},{2,10},{6,14},... | collective-permute-start | bytes 296 | tf_op jit(solution)/shard_map/ppermute | solution.py:40
  60.8 1.4 copy-start.4
  63.7 1.9 %copy-start.1 = (bf16[3072,256]{1,0:T(8,128)(2,1)S(1)}, bf16[3072,256]{1,0:T(8,128)(2,1)}, u32[]{:S(2)}) copy-start(bf16[3072,256]{1,0:T(8,128)(2,1)} %param.14) | copy-start | bytes 4718596
  105.9 1.3 slice-start
  109.9 30.2 %copy-start.2 = (u32[32]{0:T(128)S(1)}, u32[32]{0:T(128)}, u32[]{:S(2)}) copy-start(u32[32]{0:T(128)} %constant.37) | copy-start | bytes 388
  135.8 5.6 %collective-permute-start.2 = (bf16[6,3072]{1,0:T(8,128)(2,1)S(1)}, bf16[6,3072]{1,0:T(8,128)(2,1)S(1)}, u32[]{:S(2)}, u32[]{:S(2)}) collective-permute-start(bf16[6,3072]{1,0:T(8,128)(2,1)S(1)} %slice.36), channel_id=1, source_target_pairs={{0,1},{1,2},{2,3},{4,5},{5,6},{6,7},{8,9},{9,10},{10,11},{12,13},{... | collective-permute-start | bytes 110600
Sparse Core Ops, SparseCore 0:
  25.9 33.7 all-reduce.4
  63.9 33.6 all-gather.5
